TPU v7x, 32 devices: a whole 2x2x4 slice. The times are simulated.
32 devices in a mesh: row: 4 (over x, core), col: 4 (over z), pt: 2 (over y).
Axes of the slice: x: 2, y: 2, z: 4, core: 2. Of those that a mesh axis runs over, the one named last changes fastest.
Arguments:
- first_factors: int32 [32, 1024, 1024], P('pt', 'row', 'col'), may hold values from 0 to 12288
- second_factors: int32 [32, 1024, 1024], P('pt', 'row', 'col'), may hold values from 0 to 12288
Outputs:
- scaled_product: float32 [45, 1024, 1024], P(None, ('row', 'pt'), 'col')
All inputs are finite; a program needn't handle non-finite values.
Results may differ from a plain program's by a relative error of at most 0.0003.
Values may be sent and summed in bfloat16 or wider, within the bound.
A program may use at most 128 MiB of HBM per device.

v0:
```python
import jax
import jax.numpy as jnp
import numpy as np
from jax import lax
from jax.sharding import PartitionSpec as P

DEG = 16
modulus = 12289
digit_base = 128


def primitive_root():
    for candidate in range(2, modulus):
        if pow(candidate, 6144, modulus) != 1 and pow(candidate, 4096, modulus) != 1:
            return candidate
    return 0


def make_table(order_size, row_count, column_count, inverse):
    generator = primitive_root()
    root_value = pow(generator, (modulus - 1) // order_size, modulus)
    scaling = 1
    if inverse:
        root_value = pow(root_value, modulus - 2, modulus)
        scaling = pow(order_size, modulus - 2, modulus)
    entries = [
        [
            pow(root_value, row_index * column_index % order_size, modulus) * scaling % modulus
            for column_index in range(column_count)
        ]
        for row_index in range(row_count)
    ]
    return np.array(entries, dtype=np.int64)


def value_digits(values):
    high_digit = values // digit_base
    return (
        high_digit.astype(jnp.bfloat16),
        (values - digit_base * high_digit).astype(jnp.bfloat16),
    )


def combine(high_high, high_low, low_high, low_low):
    top_part = high_high.astype(jnp.int32) % modulus
    middle_part = (high_low.astype(jnp.int32) + low_high.astype(jnp.int32)) % modulus
    return (
        top_part * (digit_base * digit_base) % modulus
        + middle_part * digit_base
        + low_low.astype(jnp.int32)
    ) % modulus


def transform(matrix_table, coefs):
    slot_count = coefs.shape[0]
    flat_coefs = coefs.reshape(slot_count, -1)
    table_high = jnp.asarray(matrix_table // digit_base, dtype=jnp.bfloat16)
    table_low = jnp.asarray(matrix_table % digit_base, dtype=jnp.bfloat16)
    data_high, data_low = value_digits(flat_coefs)

    def product_of(left_part, right_part):
        return jnp.dot(left_part, right_part, preferred_element_type=jnp.float32)

    mixed_values = combine(
        product_of(table_high, data_high),
        product_of(table_high, data_low),
        product_of(table_low, data_high),
        product_of(table_low, data_low),
    )
    return mixed_values.reshape(matrix_table.shape[0], coefs.shape[1], coefs.shape[2])


def batched_product(left_part, right_part):
    return jnp.einsum("bik,bkj->bij", left_part, right_part, preferred_element_type=jnp.float32)


def digit_sum(totals, left_digits, right_digits):
    return (
        totals[0] + batched_product(left_digits[0], right_digits[0]),
        totals[1] + batched_product(left_digits[0], right_digits[1]),
        totals[2] + batched_product(left_digits[1], right_digits[0]),
        totals[3] + batched_product(left_digits[1], right_digits[1]),
    )


def pointwise(left_values, right_values):
    left_points, right_points = (
        lax.all_to_all(
            lax.all_to_all(
                left_values.astype(jnp.float32), "col", split_axis=0, concat_axis=2, tiled=True
            ),
            "pt",
            split_axis=0,
            concat_axis=1,
            tiled=True,
        ),
        lax.all_to_all(
            lax.all_to_all(
                right_values.astype(jnp.float32), "col", split_axis=0, concat_axis=2, tiled=True
            ),
            "pt",
            split_axis=0,
            concat_axis=1,
            tiled=True,
        ),
    )
    left_digits = value_digits(left_points.astype(jnp.int32))
    right_digits = value_digits(right_points.astype(jnp.int32))
    zeros_init = jnp.zeros(left_points.shape, jnp.float32)
    column_parts = tuple((digit_part for digit_part in left_digits))
    totals = digit_sum(
        (zeros_init, zeros_init, zeros_init, zeros_init),
        column_parts,
        (
            lax.all_gather(right_digits[0], "row", axis=1, tiled=True),
            lax.all_gather(right_digits[1], "row", axis=1, tiled=True),
        ),
    )
    product_values = combine(totals[0], totals[1], totals[2], totals[3]).astype(jnp.float32)
    arrived = lax.all_to_all(
        lax.all_to_all(product_values, "col", split_axis=2, concat_axis=0, tiled=True),
        "pt",
        split_axis=1,
        concat_axis=0,
        tiled=True,
    )
    col_count = lax.axis_size("col")
    pt_count = lax.axis_size("pt")
    local_count = arrived.shape[0] // (col_count * pt_count)
    returned = arrived.reshape(pt_count, col_count, local_count, arrived.shape[1], arrived.shape[2])
    returned = returned.transpose(1, 0, 2, 3, 4).reshape(arrived.shape)
    return returned.astype(jnp.int32)


def local(first_factors, second_factors):
    forward_one = make_table(2 * DEG, 2 * DEG, DEG, False)
    inverse_one = make_table(2 * DEG, 2 * DEG, 2 * DEG, True)
    forward_two = make_table(4 * DEG, 4 * DEG, 2 * DEG, False)
    inverse_two = make_table(4 * DEG, 3 * DEG - 3, 4 * DEG, True)
    first_entries, second_entries = (
        lax.all_to_all(
            first_factors.astype(jnp.float32), "pt", split_axis=1, concat_axis=0, tiled=True
        ),
        lax.all_to_all(
            second_factors.astype(jnp.float32), "pt", split_axis=1, concat_axis=0, tiled=True
        ),
    )
    first_entries = first_entries.astype(jnp.int32)
    second_entries = second_entries.astype(jnp.int32)
    left_values = jnp.concatenate(
        [transform(forward_one, first_entries[:DEG]), transform(forward_one, first_entries[DEG:])],
        0,
    )
    right_values = jnp.concatenate(
        [
            transform(forward_one, second_entries[:DEG]),
            transform(forward_one, second_entries[DEG:]),
        ],
        0,
    )
    products = pointwise(left_values, right_values)
    first_product = transform(inverse_one, products[: 2 * DEG])
    second_product = transform(inverse_one, products[2 * DEG :])
    upper_values = transform(forward_two, first_product)
    lower_values = transform(forward_two[:, :DEG], second_product[DEG:])
    result_coefficients = transform(inverse_two, pointwise(upper_values, lower_values))
    return result_coefficients.astype(jnp.float32) / 12289.0


def reduce_centred(values):
    return values - 12289.0 * jnp.round(values * (1.0 / 12289.0))


def centred_digits(values):
    high_digit = jnp.round(values * (1.0 / 128.0))
    return (high_digit.astype(jnp.bfloat16), (values - 128.0 * high_digit).astype(jnp.bfloat16))


def combine_centred(high_high, middle, low_low):
    upper_part = reduce_centred(reduce_centred(high_high) * 128.0 + middle)
    return reduce_centred(upper_part * 128.0 + low_low)


def table_digits(matrix_table):
    centred = np.where(matrix_table > modulus // 2, matrix_table - modulus, matrix_table)
    high_digit = np.round(centred / 128.0)
    return (high_digit, centred - 128.0 * high_digit)


def centred_transform(table_high, table_low, coefs):
    data_high, data_low = centred_digits(coefs.astype(jnp.float32))
    table_high = jnp.asarray(table_high, dtype=jnp.bfloat16)
    table_low = jnp.asarray(table_low, dtype=jnp.bfloat16)

    def product_of(left_part, right_part):
        return jnp.einsum("ts,sab->tab", left_part, right_part, preferred_element_type=jnp.float32)

    middle = product_of(
        jnp.concatenate([table_high, table_low], 1), jnp.concatenate([data_low, data_high], 0)
    )
    return combine_centred(
        product_of(table_high, data_high), middle, product_of(table_low, data_low)
    )


def column_pointwise(left_values, right_values):
    right_points = lax.all_to_all(
        right_values.astype(jnp.int16), "col", split_axis=0, concat_axis=2, tiled=True
    )
    right_points = lax.all_gather(right_points, "row", axis=1, tiled=True)
    left_points = lax.all_to_all(
        left_values.astype(jnp.int16), "col", split_axis=0, concat_axis=2, tiled=True
    )
    left_high, left_low = centred_digits(left_points.astype(jnp.float32))
    right_high, right_low = centred_digits(right_points.astype(jnp.float32))
    middle = batched_product(left_high, right_low) + batched_product(left_low, right_high)
    product_values = combine_centred(
        batched_product(left_high, right_high), middle, batched_product(left_low, right_low)
    )
    return lax.all_to_all(
        product_values.astype(jnp.int16), "col", split_axis=2, concat_axis=0, tiled=True
    )


def pair_local(first_factors, second_factors):
    forward_one = table_digits(make_table(2 * DEG, 2 * DEG, DEG, False))
    inverse_one = table_digits(make_table(2 * DEG, 2 * DEG, 2 * DEG, True))
    forward_two = table_digits(make_table(4 * DEG, 4 * DEG, 2 * DEG, False))
    inverse_two = table_digits(make_table(4 * DEG, 3 * DEG - 3, 4 * DEG, True))
    half_points = 2 * DEG
    place = lax.axis_index("pt")
    products = column_pointwise(
        centred_transform(*forward_one, centre(first_factors)),
        centred_transform(*forward_one, centre(second_factors)),
    )
    own_product = centred_transform(*inverse_one, products).astype(jnp.int16)
    both_products = lax.all_gather(own_product, "pt", axis=0, tiled=True)
    first_product = both_products[: 2 * DEG]
    shifted = both_products[3 * DEG :]
    own_tables = [
        lax.dynamic_slice_in_dim(
            jnp.asarray(digit, dtype=jnp.bfloat16), place * half_points, half_points, 0
        )
        for digit in forward_two
    ]
    upper_values = centred_transform(*own_tables, first_product)
    lower_values = centred_transform(*[digit[:, :DEG] for digit in own_tables], shifted)
    products_two = column_pointwise(upper_values, lower_values)
    all_points = lax.all_to_all(products_two, "pt", split_axis=1, concat_axis=0, tiled=True)
    result = centred_transform(*inverse_two, all_points)
    return jnp.where(result < 0.0, result + 12289.0, result) / 12289.0


def centre(values):
    return jnp.where(values > modulus // 2, values - modulus, values)


def solution(mesh):
    in_specs = (P("pt", "row", "col"), P("pt", "row", "col"))
    out_specs = P(None, ("row", "pt"), "col")
    body = pair_local if mesh.shape["pt"] == 2 else local
    return jax.shard_map(body, mesh=mesh, in_specs=in_specs, out_specs=out_specs, check_vma=False)
```

profile of v0, /device:TPU:0, one launch (start us, length us, event | category | flops | bytes accessed | tf_op | source)
XLA Modules:
  0.0 1258.8 jit_solution(4259190581243966023)
XLA Ops:
  0.0 5.5 fusion.68
  6.8 1.4 fusion.55
  8.2 7.1 subtract_convert_fusion.8
  15.3 4.3 copy.69
  19.6 6.6 all-to-all-start
  26.2 5.4 fusion.67
  31.7 1.4 fusion.59
  34.3 7.1 subtract_convert_fusion.7
  41.4 4.4 copy.74
  45.8 73.8 %all-to-all-done = s16[32,256,256]{2,1,0:T(8,128)(2,1)} async-done(((s16[32,256,256]{2,1,0:T(8,128)(2,1)}), s16[32,256,256]{2,1,0:T(8,128)(2,1)}, u32[]{:S(2)}, u32[]{:S(2)}) %all-to-all-start) | async-done | bytes 4194336 | tf_op jit(solution)/shard_map/all_to_all | solution.py:211
  119.6 5.3 all-to-all-start.1
  124.9 6.8 convert.12
  131.8 12.0 copy.111
  143.8 10.8 reshape.16
  154.6 63.0 %all-to-all-done.1 = s16[32,256,256]{2,1,0:T(8,128)(2,1)} async-done(((s16[32,256,256]{2,1,0:T(8,128)(2,1)}), s16[32,256,256]{2,1,0:T(8,128)(2,1)}, u32[]{:S(2)}, u32[]{:S(2)}) %all-to-all-start.1) | async-done | bytes 4194336 | tf_op jit(solution)/shard_map/all_to_all | solution.py:207
  217.6 7.4 copy.113
  225.0 7.9 all_to_all.71
  232.9 105.4 %all-gather.3 = s16[8,1024,1024]{2,1,0:T(8,128)(2,1)} all-gather(s16[8,256,1024]{2,1,0:T(8,128)(2,1)} %all_to_all.71), channel_id=1, replica_groups=mesh['row'=4,'col'=4,'pt'=2] {'row'}, dimensions={1}, use_global_device_ids=true | all-gather | bytes 20971520 | tf_op jit(solution)/shard_map/all_gather | solution.py:210
  338.4 16.5 %fusion.14 = f32[8,256,1024]{2,1,0:T(8,128)} fusion(s16[8,1024,1024]{2,1,0:T(8,128)(2,1)} %all-gather.3, f32[8,256,1024]{2,1,0:T(8,128)} %reshape.16), kind=kOutput, calls=%fused_computation.16 | convolution fusion | flops 4334813184 | bytes 33554432 | tf_op jit(solution)/shard_map/bik,bkj->bij/dot_general | solution.py:74
  354.9 17.6 %fusion.12 = f32[8,256,1024]{2,1,0:T(8,128)} fusion(s16[8,1024,1024]{2,1,0:T(8,128)(2,1)} %all-gather.3, f32[8,256,1024]{2,1,0:T(8,128)} %reshape.16), kind=kOutput, calls=%fused_computation.15 | convolution fusion | flops 4339007488 | bytes 33554432 | tf_op jit(solution)/shard_map/bik,bkj->bij/dot_general | solution.py:74
  372.5 18.3 %fusion.20 = f32[8,256,1024]{2,1,0:T(8,128)} fusion(s16[8,1024,1024]{2,1,0:T(8,128)(2,1)} %all-gather.3, f32[8,256,1024]{2,1,0:T(8,128)} %reshape.16), kind=kOutput, calls=%fused_computation.23 | convolution fusion | flops 4355784704 | bytes 33554432 | tf_op jit(solution)/shard_map/bik,bkj->bij/dot_general | solution.py:74
  390.8 25.6 %subtract_convert_fusion.5 = s16[8,256,1024]{2,1,0:T(8,128)(2,1)} fusion(f32[8,256,1024]{2,1,0:T(8,128)} %fusion.20, f32[8,256,1024]{2,1,0:T(8,128)} %fusion.12, f32[8,256,1024]{2,1,0:T(8,128)} %fusion.14, s16[8,1024,1024]{2,1,0:T(8,128)(2,1)} %all-gather.3, f32[8,256,1024]{2,1,0:T(8,128)} %reshape.16), kind=kOutput, calls=%fused_computation.59 | convolution fusion | flops 4389339136 | bytes 54525952 | tf_op jit(solution)/shard_map/bik,bkj->bij/dot_general | solution.py:74
  416.3 7.3 copy.76
  423.6 5.1 all-to-all-start.2
  428.8 94.0 %all-to-all-done.2 = s16[8,256,1024]{1,0,2:T(8,128)(2,1)} async-done(((s16[8,256,1024]{1,0,2:T(8,128)(2,1)}), s16[8,256,1024]{1,0,2:T(8,128)(2,1)}, u32[]{:S(2)}, u32[]{:S(2)}) %all-to-all-start.2) | async-done | bytes 4194336 | tf_op jit(solution)/shard_map/all_to_all | solution.py:220
  522.8 6.5 convert.13
  529.3 10.5 copy.77
  539.8 4.5 fusion.46
  545.5 1.5 fusion.28
  547.0 8.1 subtract_convert_fusion.4
  555.1 92.8 %all-gather.4 = s16[64,256,256]{2,0,1:T(8,128)(2,1)S(1)} all-gather(s16[32,256,256]{2,0,1:T(8,128)(2,1)} %subtract_convert_fusion.4), channel_id=1, replica_groups=mesh['row'=4,'col'=4,'pt'=2] {'pt'}, dimensions={0}, use_global_device_ids=true | all-gather | bytes 12582912 | tf_op jit(solution)/shard_map/all_gather | solution.py:237
  648.0 3.1 fusion.27
  651.1 4.6 fusion.84
  657.1 10.0 subtract_convert_fusion.3
  667.0 4.3 copy.78
  671.3 5.1 all-to-all-start.3
  676.4 3.0 fusion.52
  682.9 8.5 subtract_convert_fusion.2
  691.5 6.5 copy.82
  698.0 70.7 %all-to-all-done.3 = s16[32,256,256]{2,1,0:T(8,128)(2,1)} async-done(((s16[32,256,256]{2,1,0:T(8,128)(2,1)}), s16[32,256,256]{2,1,0:T(8,128)(2,1)}, u32[]{:S(2)}, u32[]{:S(2)}) %all-to-all-start.3) | async-done | bytes 4194336 | tf_op jit(solution)/shard_map/all_to_all | solution.py:211
  768.7 5.1 all-to-all-start.4
  773.8 6.8 convert.14
  780.6 12.0 copy.110
  792.6 10.8 reshape.18
  803.4 63.1 %all-to-all-done.4 = s16[32,256,256]{2,1,0:T(8,128)(2,1)} async-done(((s16[32,256,256]{2,1,0:T(8,128)(2,1)}), s16[32,256,256]{2,1,0:T(8,128)(2,1)}, u32[]{:S(2)}, u32[]{:S(2)}) %all-to-all-start.4) | async-done | bytes 4194336 | tf_op jit(solution)/shard_map/all_to_all | solution.py:207
  866.5 7.4 copy.112
  874.0 7.9 all_to_all.77
  881.9 104.5 %all-gather.5 = s16[8,1024,1024]{2,1,0:T(8,128)(2,1)} all-gather(s16[8,256,1024]{2,1,0:T(8,128)(2,1)} %all_to_all.77), channel_id=1, replica_groups=mesh['row'=4,'col'=4,'pt'=2] {'row'}, dimensions={1}, use_global_device_ids=true | all-gather | bytes 20971520 | tf_op jit(solution)/shard_map/all_gather | solution.py:210
  986.4 16.5 %fusion.10 = f32[8,256,1024]{2,1,0:T(8,128)} fusion(s16[8,1024,1024]{2,1,0:T(8,128)(2,1)} %all-gather.5, f32[8,256,1024]{2,1,0:T(8,128)} %reshape.18), kind=kOutput, calls=%fused_computation.14 | convolution fusion | flops 4334813184 | bytes 33554432 | tf_op jit(solution)/shard_map/bik,bkj->bij/dot_general | solution.py:74
  1002.9 17.6 %fusion.8 = f32[8,256,1024]{2,1,0:T(8,128)} fusion(s16[8,1024,1024]{2,1,0:T(8,128)(2,1)} %all-gather.5, f32[8,256,1024]{2,1,0:T(8,128)} %reshape.18), kind=kOutput, calls=%fused_computation.13 | convolution fusion | flops 4339007488 | bytes 33554432 | tf_op jit(solution)/shard_map/bik,bkj->bij/dot_general | solution.py:74
  1020.5 18.3 %fusion.16 = f32[8,256,1024]{2,1,0:T(8,128)} fusion(s16[8,1024,1024]{2,1,0:T(8,128)(2,1)} %all-gather.5, f32[8,256,1024]{2,1,0:T(8,128)} %reshape.18), kind=kOutput, calls=%fused_computation.21 | convolution fusion | flops 4355784704 | bytes 33554432 | tf_op jit(solution)/shard_map/bik,bkj->bij/dot_general | solution.py:74
  1038.7 25.6 %subtract_convert_fusion = s16[8,256,1024]{2,1,0:T(8,128)(2,1)} fusion(f32[8,256,1024]{2,1,0:T(8,128)} %fusion.16, f32[8,256,1024]{2,1,0:T(8,128)} %fusion.8, f32[8,256,1024]{2,1,0:T(8,128)} %fusion.10, s16[8,1024,1024]{2,1,0:T(8,128)(2,1)} %all-gather.5, f32[8,256,1024]{2,1,0:T(8,128)} %reshape.18), kind=kOutput, calls=%fused_computation.52 | convolution fusion | flops 4389339136 | bytes 54525952 | tf_op jit(solution)/shard_map/bik,bkj->bij/dot_general | solution.py:74
  1064.3 7.3 copy.84
  1071.5 99.7 %all_to_all.90 = s16[8,256,1024]{1,0,2:T(8,128)(2,1)} all-to-all(s16[8,256,1024]{1,0,2:T(8,128)(2,1)} %copy.84), channel_id=1, replica_groups=mesh['row'=4,'col'=4,'pt'=2] {'col'}, dimensions={2} | all-to-all | bytes 8388608 | tf_op jit(solution)/shard_map/all_to_all | solution.py:220
  1171.2 7.9 copy.86
  1179.1 4.5 copy.87
  1183.6 50.0 %all_to_all.91 = s16[32,256,256]{2,0,1:T(8,128)(2,1)S(1)} all-to-all(s16[32,256,256]{2,0,1:T(8,128)(2,1)S(1)} %copy.87), channel_id=1, replica_groups=mesh['row'=4,'col'=4,'pt'=2] {'pt'}, dimensions={1} | all-to-all | bytes 8388608 | tf_op jit(solution)/shard_map/all_to_all | solution.py:249
  1233.6 2.4 copy.88
  1236.0 1.4 convert_bitcast_fusion
  1237.4 4.9 copy.89
  1242.3 2.1 fusion.41
  1245.4 1.5 fusion.36
  1246.9 5.5 fusion.48
  1252.4 6.0 copy.90
  (38 shorter events, 9.6 us)
Async XLA Ops:
  0.0 5.5 copy-start.3
  0.0 6.8 copy-start.2
  6.7 1.4 copy-start.11
  19.6 100.0 %all-to-all-start = ((s16[32,256,256]{2,1,0:T(8,128)(2,1)}), s16[32,256,256]{2,1,0:T(8,128)(2,1)}, u32[]{:S(2)}, u32[]{:S(2)}) async-start(s16[32,256,256]{2,1,0:T(8,128)(2,1)} %copy.69), calls=%async_computation | async-start | bytes 8388608 | tf_op jit(solution)/shard_map/all_to_all | solution.py:211
  119.6 98.0 %all-to-all-start.1 = ((s16[32,256,256]{2,1,0:T(8,128)(2,1)}), s16[32,256,256]{2,1,0:T(8,128)(2,1)}, u32[]{:S(2)}, u32[]{:S(2)}) async-start(s16[32,256,256]{2,1,0:T(8,128)(2,1)} %copy.74), calls=%async_computation.1 | async-start | bytes 8388608 | tf_op jit(solution)/shard_map/all_to_all | solution.py:207
  416.3 12.5 copy-start.1
  416.3 12.5 copy-start.4
  423.6 99.2 %all-to-all-start.2 = ((s16[8,256,1024]{1,0,2:T(8,128)(2,1)}), s16[8,256,1024]{1,0,2:T(8,128)(2,1)}, u32[]{:S(2)}, u32[]{:S(2)}) async-start(s16[8,256,1024]{1,0,2:T(8,128)(2,1)} %copy.76), calls=%async_computation.2 | async-start | bytes 8388608 | tf_op jit(solution)/shard_map/all_to_all | solution.py:220
  539.8 4.5 copy-start.8
  544.3 1.3 copy-start.7
  545.5 1.5 copy-start.10
  648.0 9.1 copy-start
  671.3 97.4 %all-to-all-start.3 = ((s16[32,256,256]{2,1,0:T(8,128)(2,1)}), s16[32,256,256]{2,1,0:T(8,128)(2,1)}, u32[]{:S(2)}, u32[]{:S(2)}) async-start(s16[32,256,256]{2,1,0:T(8,128)(2,1)} %copy.78), calls=%async_computation.3 | async-start | bytes 8388608 | tf_op jit(solution)/shard_map/all_to_all | solution.py:211
  676.4 4.3 slice-start
  679.4 2.2 slice-start.1
  768.7 97.8 %all-to-all-start.4 = ((s16[32,256,256]{2,1,0:T(8,128)(2,1)}), s16[32,256,256]{2,1,0:T(8,128)(2,1)}, u32[]{:S(2)}, u32[]{:S(2)}) async-start(s16[32,256,256]{2,1,0:T(8,128)(2,1)} %copy.82), calls=%async_computation.4 | async-start | bytes 8388608 | tf_op jit(solution)/shard_map/all_to_all | solution.py:207
  1242.3 2.2 copy-start.5
  1244.4 1.0 copy-start.6
  1245.4 1.5 copy-start.9
where the time goes:
time: 1270 us; the launch traced here: 1260 us
  blocking collectives  452 us (36%)
  waiting for transfers between devices  364 us (29%)
  matrix products  221 us (17%)
  local copies, waits for them, and re-layouts  148 us (12%)
  other arithmetic  45.2 us (4%)
  starting transfers between devices  27.2 us (2%)
    all_gather x2, blocking collectives, column_pointwise(): right_points = lax.all_gather(right_points, 'row', axis=1, tiled=True)  210 us
    dot_general x8, matrix products, batched_product(): jnp.einsum('bik,bkj->bij', left_part, right_part, preferred_element_type=...  156 us
    all_to_all x2, waiting for transfers between devices, column_pointwise(): lax.all_to_all(left_values.astype(jnp.int16), 'col', split_axis=0, concat...  144 us
    all_to_all x2, waiting for transfers between devices, column_pointwise(): lax.all_to_all(right_values.astype(jnp.int16), 'col', split_axis=0, conca...  126 us
    all_to_all x1, blocking collectives, column_pointwise(): lax.all_to_all(product_values.astype(jnp.int16), 'col', split_axis=2, con...  99.7 us
    all_to_all x1, waiting for transfers between devices, column_pointwise(): lax.all_to_all(product_values.astype(jnp.int16), 'col', split_axis=2, con...  94 us
    all_gather x1, blocking collectives, pair_local(): both_products = lax.all_gather(own_product, 'pt', axis=0, tiled=True)  92.8 us
    dot_general x18, matrix products, product_of(): jnp.einsum('ts,sab->tab', left_part, right_part, preferred_element_type=j...  65.3 us
  transfers between devices with their start and end apart: 5, of which 5 were waited for; matrix products, arithmetic and copies ran while one was open for 8% of the time, Pallas kernels for 0%

commit v1 on v0

--- a/solution.py
+++ b/solution.py
@@ -7,6 +7,18 @@
 DEG = 16
 modulus = 12289
 digit_base = 128
+
+
+def rotated_exchange(shard, axis, split, join):
+    ways, here = (lax.axis_size(axis), lax.axis_index(axis))
+    width = shard.shape[split] // ways
+    turned = jnp.roll(shard, -here * width, axis=split)
+    got = [lax.slice_in_dim(turned, 0, width, axis=split)]
+    for far in range(1, ways):
+        sent = lax.slice_in_dim(turned, far * width, (far + 1) * width, axis=split)
+        got.append(lax.ppermute(sent, axis, [(d, (d + far) % ways) for d in range(ways)]))
+    line = jnp.concatenate(got[::-1], axis=join)
+    return jnp.roll(line, (here + 1) * got[0].shape[join], axis=join)
 
 
 def primitive_root():
@@ -208,9 +220,7 @@
         right_values.astype(jnp.int16), "col", split_axis=0, concat_axis=2, tiled=True
     )
     right_points = lax.all_gather(right_points, "row", axis=1, tiled=True)
-    left_points = lax.all_to_all(
-        left_values.astype(jnp.int16), "col", split_axis=0, concat_axis=2, tiled=True
-    )
+    left_points = rotated_exchange(left_values.astype(jnp.int16), "col", 0, 2)
     left_high, left_low = centred_digits(left_points.astype(jnp.float32))
     right_high, right_low = centred_digits(right_points.astype(jnp.float32))
     middle = batched_product(left_high, right_low) + batched_product(left_low, right_high)

time: 1270 us -> 1350 us (1.063)
  other arithmetic: 45.2 us -> 128 us
  local copies, waits for them, and re-layouts: 148 us -> 91.6 us
  waiting for transfers between devices: 364 us -> 407 us
    ppermute x0 -> x6, waiting for transfers between devices: none -> 313 us  [rotated_exchange(): lax.ppermute(sent, axis, [(d, (d + far) % ways) for d in range(ways)])]
    all_to_all x2 -> x0, waiting for transfers between devices: 144 us -> none  [column_pointwise(): lax.all_to_all(left_values.astype(jnp.int16), 'col', split_axis=0, concat...]
    all_to_all x2, waiting for transfers between devices: 126 us -> 0.01 us  [column_pointwise(): lax.all_to_all(right_values.astype(jnp.int16), 'col', split_axis=0, conca...]
    convert_element_type x6 -> x0, local copies, waits for them, and re-layouts: 54.3 us -> none  [the longest x4 45.7 us: column_pointwise(): left_high, left_low = centred_digits(left_points.astype(jnp.float32))]
    convert_element_type x2, other arithmetic: 13.6 us -> 66.9 us  [column_pointwise(): product_values.astype(jnp.int16)]
    convert_element_type x3 -> x5, other arithmetic: 15.4 us -> 32.1 us  [centred_digits(): high_digit.astype(jnp.bfloat16)]
  transfers between devices with their start and end apart: 5 -> 9, of which waited for: 5 -> 5; matrix products, arithmetic and copies ran while one was open for 8% -> 5% of each run, Pallas kernels for 0% -> 0%
where the time goes in v1:
time: 1350 us; the launch traced here: 1340 us
  blocking collectives  453 us (34%)
  waiting for transfers between devices  407 us (30%)
  matrix products  230 us (17%)
  other arithmetic  128 us (9%)
  local copies, waits for them, and re-layouts  91.6 us (7%)
  starting transfers between devices  26.7 us (2%)
    ppermute x6, waiting for transfers between devices, rotated_exchange(): lax.ppermute(sent, axis, [(d, (d + far) % ways) for d in range(ways)])  313 us
    all_gather x2, blocking collectives, column_pointwise(): right_points = lax.all_gather(right_points, 'row', axis=1, tiled=True)  210 us
    dot_general x8, matrix products, batched_product(): jnp.einsum('bik,bkj->bij', left_part, right_part, preferred_element_type=...  167 us
    all_to_all x1, blocking collectives, column_pointwise(): lax.all_to_all(product_values.astype(jnp.int16), 'col', split_axis=2, con...  99.7 us
    all_to_all x1, waiting for transfers between devices, column_pointwise(): lax.all_to_all(product_values.astype(jnp.int16), 'col', split_axis=2, con...  94 us
    all_gather x1, blocking collectives, pair_local(): both_products = lax.all_gather(own_product, 'pt', axis=0, tiled=True)  92.9 us
    convert_element_type x2, other arithmetic, column_pointwise(): product_values.astype(jnp.int16)  66.9 us
    dot_general x18, matrix products, product_of(): jnp.einsum('ts,sab->tab', left_part, right_part, preferred_element_type=j...  62.8 us
  transfers between devices with their start and end apart: 9, of which 5 were waited for; matrix products, arithmetic and copies ran while one was open for 5% of the time, Pallas kernels for 0%

profile of v1, /device:TPU:0, one launch (start us, length us, event | category | flops | bytes accessed | tf_op | source)
XLA Modules:
  0.0 1337.4 jit_solution(302708210319452011)
XLA Ops:
  0.0 5.5 fusion.91
  6.8 1.4 fusion.83
  8.2 7.1 subtract_convert_fusion.5
  15.3 4.4 copy.116
  19.7 6.5 all-to-all-start
  26.2 5.4 fusion.92
  31.7 1.4 fusion.79
  34.4 7.1 subtract_convert_fusion.6
  41.4 2.3 fusion.76
  43.7 1.9 fusion.136
  45.6 3.8 collective-permute-start
  50.8 66.8 %collective-permute-done = s16[8,256,256]{2,0,1:T(8,128)(2,1)S(1)} collective-permute-done((s16[8,256,256]{2,0,1:T(8,128)(2,1)}, s16[8,256,256]{2,0,1:T(8,128)(2,1)S(1)}, u32[]{:S(2)}, u32[]{:S(2)}) %collective-permute-start) | collective-permute-done | bytes 1048608 | tf_op jit(solution)/shard_map/ppermute | solution.py:19
  117.5 91.9 %collective-permute-done.1 = s16[8,256,256]{2,0,1:T(8,128)(2,1)S(1)} collective-permute-done((s16[8,256,256]{2,0,1:T(8,128)(2,1)}, s16[8,256,256]{2,0,1:T(8,128)(2,1)S(1)}, u32[]{:S(2)}, u32[]{:S(2)}) %collective-permute-start.1) | collective-permute-done | bytes 1048608 | tf_op jit(solution)/shard_map/ppermute | solution.py:19
  209.4 8.7 fusion.26
  218.1 3.7 fusion.27
  221.8 7.4 copy.204
  229.3 7.8 all_to_all.56
  237.1 105.3 %all-gather.3 = s16[8,1024,1024]{2,1,0:T(8,128)(2,1)} all-gather(s16[8,256,1024]{2,1,0:T(8,128)(2,1)} %all_to_all.56), channel_id=1, replica_groups=mesh['row'=4,'col'=4,'pt'=2] {'row'}, dimensions={1}, use_global_device_ids=true | all-gather | bytes 20971520 | tf_op jit(solution)/shard_map/all_gather | solution.py:222
  342.4 18.7 %fusion.14 = f32[8,256,1024]{2,1,0:T(8,128)S(1)} fusion(s16[8,1024,1024]{2,1,0:T(8,128)(2,1)} %all-gather.3, bf16[8,256,1024]{2,0,1:T(8,128)(2,1)} %get-tuple-element.9), kind=kOutput, calls=%fused_computation.16 | convolution fusion | flops 4328521728 | bytes 29360128 | tf_op jit(solution)/shard_map/bik,bkj->bij/dot_general | solution.py:86
  361.1 22.1 %fusion.22 = f32[8,256,1024]{2,1,0:T(8,128)} fusion(s16[8,1024,1024]{2,1,0:T(8,128)(2,1)} %all-gather.3, bf16[8,256,1024]{2,0,1:T(8,128)(2,1)} %get-tuple-element.9), kind=kOutput, calls=%fused_computation.28 | convolution fusion | flops 4345298944 | bytes 29360128 | tf_op jit(solution)/shard_map/bik,bkj->bij/dot_general | solution.py:86
  383.3 20.8 %fusion.12 = f32[8,256,1024]{2,1,0:T(8,128)} fusion(s16[8,1024,1024]{2,1,0:T(8,128)(2,1)} %all-gather.3, bf16[8,256,1024]{2,0,1:T(8,128)(2,1)} %fusion.27), kind=kOutput, calls=%fused_computation.15 | convolution fusion | flops 4328521728 | bytes 29360128 | tf_op jit(solution)/shard_map/bik,bkj->bij/dot_general | solution.py:86
  404.1 21.8 %fusion.20 = f32[8,256,1024]{2,1,0:T(8,128)} fusion(s16[8,1024,1024]{2,1,0:T(8,128)(2,1)} %all-gather.3, bf16[8,256,1024]{2,0,1:T(8,128)(2,1)} %fusion.27), kind=kOutput, calls=%fused_computation.27 | convolution fusion | flops 4345298944 | bytes 29360128 | tf_op jit(solution)/shard_map/bik,bkj->bij/dot_general | solution.py:86
  425.9 33.4 %subtract_convert_fusion.4 = s16[8,256,1024]{2,0,1:T(8,128)(2,1)} fusion(f32[8,256,1024]{2,1,0:T(8,128)} %fusion.20, f32[8,256,1024]{2,1,0:T(8,128)} %fusion.12, f32[8,256,1024]{2,1,0:T(8,128)} %fusion.22, f32[8,256,1024]{2,1,0:T(8,128)S(1)} %fusion.14), kind=kLoop, calls=%fused_computation.92 | loop fusion | flops 37748736 | bytes 37748736 | tf_op jit(solution)/shard_map/convert_element_type | solution.py:231
  459.2 7.4 copy.127
  466.6 5.3 all-to-all-start.1
  472.0 94.0 %all-to-all-done.1 = s16[8,256,1024]{1,0,2:T(8,128)(2,1)} async-done(((s16[8,256,1024]{1,0,2:T(8,128)(2,1)}), s16[8,256,1024]{1,0,2:T(8,128)(2,1)}, u32[]{:S(2)}, u32[]{:S(2)}) %all-to-all-start.1) | async-done | bytes 4194336 | tf_op jit(solution)/shard_map/all_to_all | solution.py:230
  566.0 6.6 convert.6
  572.5 10.5 copy.128
  583.0 4.5 fusion.54
  588.8 1.5 fusion.36
  590.3 8.1 subtract_convert_fusion.3
  598.4 92.9 %all-gather.4 = s16[64,256,256]{2,0,1:T(8,128)(2,1)S(1)} all-gather(s16[32,256,256]{2,0,1:T(8,128)(2,1)} %subtract_convert_fusion.3), channel_id=1, replica_groups=mesh['row'=4,'col'=4,'pt'=2] {'pt'}, dimensions={0}, use_global_device_ids=true | all-gather | bytes 12582912 | tf_op jit(solution)/shard_map/all_gather | solution.py:247
  695.1 8.7 subtract_convert_fusion.1
  703.8 6.6 copy.131
  710.4 4.8 all-to-all-start.2
  715.3 4.4 fusion.31
  719.7 1.3 fusion.40
  721.9 2.6 fusion.108
  724.5 9.3 subtract_convert_fusion.2
  733.8 3.6 fusion.68
  737.7 3.8 collective-permute-start.3
  742.6 63.9 %collective-permute-done.3 = s16[8,256,256]{2,0,1:T(8,128)(2,1)S(1)} collective-permute-done((s16[8,256,256]{2,0,1:T(8,128)(2,1)S(1)}, s16[8,256,256]{2,0,1:T(8,128)(2,1)S(1)}, u32[]{:S(2)}, u32[]{:S(2)}) %collective-permute-start.3) | collective-permute-done | bytes 1048608 | tf_op jit(solution)/shard_map/ppermute | solution.py:19
  806.5 90.8 %collective-permute-done.4 = s16[8,256,256]{2,0,1:T(8,128)(2,1)S(1)} collective-permute-done((s16[8,256,256]{2,0,1:T(8,128)(2,1)S(1)}, s16[8,256,256]{2,0,1:T(8,128)(2,1)S(1)}, u32[]{:S(2)}, u32[]{:S(2)}) %collective-permute-start.4) | collective-permute-done | bytes 1048608 | tf_op jit(solution)/shard_map/ppermute | solution.py:19
  897.3 8.1 fusion.34
  905.4 3.7 fusion.35
  909.1 7.4 copy.203
  916.6 7.8 all_to_all.61
  924.4 104.2 %all-gather.5 = s16[8,1024,1024]{2,1,0:T(8,128)(2,1)} all-gather(s16[8,256,1024]{2,1,0:T(8,128)(2,1)} %all_to_all.61), channel_id=1, replica_groups=mesh['row'=4,'col'=4,'pt'=2] {'row'}, dimensions={1}, use_global_device_ids=true | all-gather | bytes 20971520 | tf_op jit(solution)/shard_map/all_gather | solution.py:222
  1028.6 18.7 %fusion.10 = f32[8,256,1024]{2,1,0:T(8,128)S(1)} fusion(s16[8,1024,1024]{2,1,0:T(8,128)(2,1)} %all-gather.5, bf16[8,256,1024]{2,0,1:T(8,128)(2,1)} %get-tuple-element.6), kind=kOutput, calls=%fused_computation.14 | convolution fusion | flops 4328521728 | bytes 29360128 | tf_op jit(solution)/shard_map/bik,bkj->bij/dot_general | solution.py:86
  1047.3 22.1 %fusion.18 = f32[8,256,1024]{2,1,0:T(8,128)} fusion(s16[8,1024,1024]{2,1,0:T(8,128)(2,1)} %all-gather.5, bf16[8,256,1024]{2,0,1:T(8,128)(2,1)} %get-tuple-element.6), kind=kOutput, calls=%fused_computation.26 | convolution fusion | flops 4345298944 | bytes 29360128 | tf_op jit(solution)/shard_map/bik,bkj->bij/dot_general | solution.py:86
  1069.4 20.8 %fusion.8 = f32[8,256,1024]{2,1,0:T(8,128)} fusion(s16[8,1024,1024]{2,1,0:T(8,128)(2,1)} %all-gather.5, bf16[8,256,1024]{2,0,1:T(8,128)(2,1)} %fusion.35), kind=kOutput, calls=%fused_computation.13 | convolution fusion | flops 4328521728 | bytes 29360128 | tf_op jit(solution)/shard_map/bik,bkj->bij/dot_general | solution.py:86
  1090.3 21.8 %fusion.16 = f32[8,256,1024]{2,1,0:T(8,128)} fusion(s16[8,1024,1024]{2,1,0:T(8,128)(2,1)} %all-gather.5, bf16[8,256,1024]{2,0,1:T(8,128)(2,1)} %fusion.35), kind=kOutput, calls=%fused_computation.25 | convolution fusion | flops 4345298944 | bytes 29360128 | tf_op jit(solution)/shard_map/bik,bkj->bij/dot_general | solution.py:86
  1112.0 33.5 %subtract_convert_fusion = s16[8,256,1024]{2,0,1:T(8,128)(2,1)} fusion(f32[8,256,1024]{2,1,0:T(8,128)} %fusion.16, f32[8,256,1024]{2,1,0:T(8,128)} %fusion.8, f32[8,256,1024]{2,1,0:T(8,128)} %fusion.18, f32[8,256,1024]{2,1,0:T(8,128)S(1)} %fusion.10), kind=kLoop, calls=%fused_computation.88 | loop fusion | flops 37748736 | bytes 37748736 | tf_op jit(solution)/shard_map/convert_element_type | solution.py:231
  1145.6 7.4 copy.142
  1152.9 99.7 %all_to_all.72 = s16[8,256,1024]{1,0,2:T(8,128)(2,1)} all-to-all(s16[8,256,1024]{1,0,2:T(8,128)(2,1)} %copy.142), channel_id=1, replica_groups=mesh['row'=4,'col'=4,'pt'=2] {'col'}, dimensions={2} | all-to-all | bytes 8388608 | tf_op jit(solution)/shard_map/all_to_all | solution.py:230
  1252.6 8.6 copy.143
  1261.2 51.3 %all_to_all.73 = s16[32,256,256]{2,0,1:T(8,128)(2,1)S(1)} all-to-all(s16[32,256,256]{2,0,1:T(8,128)(2,1)} %bitcast.95), channel_id=1, replica_groups=mesh['row'=4,'col'=4,'pt'=2] {'pt'}, dimensions={1} | all-to-all | bytes 8388608 | tf_op jit(solution)/shard_map/all_to_all | solution.py:259
  1312.5 2.4 copy.144
  1314.9 1.4 convert_bitcast_fusion
  1316.3 4.9 copy.145
  1321.1 2.1 fusion.49
  1324.3 1.5 fusion.44
  1325.8 5.4 fusion.56
  1331.2 6.0 copy.146
  (47 shorter events, 12.3 us)
Async XLA Ops:
  0.0 5.5 copy-start.3
  0.0 6.8 copy-start.2
  6.7 1.4 copy-start.11
  19.7 202.2 %all-to-all-start = ((s16[32,256,256]{2,1,0:T(8,128)(2,1)}), s16[32,256,256]{2,1,0:T(8,128)(2,1)}, u32[]{:S(2)}, u32[]{:S(2)}) async-start(s16[32,256,256]{2,1,0:T(8,128)(2,1)} %copy.116), calls=%async_computation | async-start | bytes 8388608 | tf_op jit(solution)/shard_map/all_to_all | solution.py:219
  45.6 72.0 %collective-permute-start = (s16[8,256,256]{2,0,1:T(8,128)(2,1)}, s16[8,256,256]{2,0,1:T(8,128)(2,1)S(1)}, u32[]{:S(2)}, u32[]{:S(2)}) collective-permute-start(s16[8,256,256]{2,0,1:T(8,128)(2,1)} %get-tuple-element.23), channel_id=1, source_target_pairs={{0,6},{2,0},{4,2},{6,4},{1,7},{3,1},{5,3},{7,5},{8,14},{10,8},{12,... | collective-permute-start | bytes 3145736 | tf_op jit(solution)/shard_map/ppermute | solution.py:19
  49.4 160.0 %collective-permute-start.1 = (s16[8,256,256]{2,0,1:T(8,128)(2,1)}, s16[8,256,256]{2,0,1:T(8,128)(2,1)S(1)}, u32[]{:S(2)}, u32[]{:S(2)}) collective-permute-start(s16[8,256,256]{2,0,1:T(8,128)(2,1)} %get-tuple-element.25), channel_id=1, source_target_pairs={{0,4},{2,6},{4,0},{6,2},{1,5},{3,7},{5,1},{7,3},{8,12},{10,14},{12... | collective-permute-start | bytes 3145736 | tf_op jit(solution)/shard_map/ppermute | solution.py:19
  49.4 160.0 %collective-permute-start.2 = (s16[8,256,256]{2,0,1:T(8,128)(2,1)}, s16[8,256,256]{2,0,1:T(8,128)(2,1)}, u32[]{:S(2)}, u32[]{:S(2)}) collective-permute-start(s16[8,256,256]{2,0,1:T(8,128)(2,1)} %get-tuple-element.24), channel_id=1, source_target_pairs={{0,2},{2,4},{4,6},{6,0},{1,3},{3,5},{5,7},{7,1},{8,10},{10,12},{12... | collective-permute-start | bytes 3145736 | tf_op jit(solution)/shard_map/ppermute | solution.py:19
  459.2 12.8 copy-start.1
  459.2 12.8 copy-start.4
  466.6 99.3 %all-to-all-start.1 = ((s16[8,256,1024]{1,0,2:T(8,128)(2,1)}), s16[8,256,1024]{1,0,2:T(8,128)(2,1)}, u32[]{:S(2)}, u32[]{:S(2)}) async-start(s16[8,256,1024]{1,0,2:T(8,128)(2,1)} %copy.127), calls=%async_computation.1 | async-start | bytes 8388608 | tf_op jit(solution)/shard_map/all_to_all | solution.py:230
  583.0 4.5 copy-start.8
  587.5 1.3 copy-start.7
  588.8 1.5 copy-start.10
  691.2 3.9 copy-start
  710.4 198.7 %all-to-all-start.2 = ((s16[32,256,256]{2,1,0:T(8,128)(2,1)}), s16[32,256,256]{2,1,0:T(8,128)(2,1)}, u32[]{:S(2)}, u32[]{:S(2)}) async-start(s16[32,256,256]{2,1,0:T(8,128)(2,1)} %copy.131), calls=%async_computation.2 | async-start | bytes 8388608 | tf_op jit(solution)/shard_map/all_to_all | solution.py:219
  715.3 5.8 slice-start
  719.7 2.2 slice-start.1
  737.7 68.8 %collective-permute-start.3 = (s16[8,256,256]{2,0,1:T(8,128)(2,1)S(1)}, s16[8,256,256]{2,0,1:T(8,128)(2,1)S(1)}, u32[]{:S(2)}, u32[]{:S(2)}) collective-permute-start(s16[8,256,256]{2,0,1:T(8,128)(2,1)S(1)} %get-tuple-element.19), channel_id=1, source_target_pairs={{0,6},{2,0},{4,2},{6,4},{1,7},{3,1},{5,3},{7,5},{8,14},{10,8},{12,... | collective-permute-start | bytes 3145736 | tf_op jit(solution)/shard_map/ppermute | solution.py:19
  741.5 155.8 %collective-permute-start.4 = (s16[8,256,256]{2,0,1:T(8,128)(2,1)S(1)}, s16[8,256,256]{2,0,1:T(8,128)(2,1)S(1)}, u32[]{:S(2)}, u32[]{:S(2)}) collective-permute-start(s16[8,256,256]{2,0,1:T(8,128)(2,1)S(1)} %get-tuple-element.21), channel_id=1, source_target_pairs={{0,4},{2,6},{4,0},{6,2},{1,5},{3,7},{5,1},{7,3},{8,12},{10,14},{12... | collective-permute-start | bytes 3145736 | tf_op jit(solution)/shard_map/ppermute | solution.py:19
  741.5 155.8 %collective-permute-start.5 = (s16[8,256,256]{2,0,1:T(8,128)(2,1)S(1)}, s16[8,256,256]{2,0,1:T(8,128)(2,1)S(1)}, u32[]{:S(2)}, u32[]{:S(2)}) collective-permute-start(s16[8,256,256]{2,0,1:T(8,128)(2,1)S(1)} %get-tuple-element.20), channel_id=1, source_target_pairs={{0,2},{2,4},{4,6},{6,0},{1,3},{3,5},{5,7},{7,1},{8,10},{10,12},{12... | collective-permute-start | bytes 3145736 | tf_op jit(solution)/shard_map/ppermute | solution.py:19
  1321.1 2.2 copy-start.5
  1323.3 1.0 copy-start.6
  1324.3 1.5 copy-start.9
